TPU v7x, 32 devices: a whole 2x2x4 slice. The times are simulated.
32 devices in a mesh: grp: 2 (over y), gx: 4 (over x, core), gy: 4 (over z).
Axes of the slice: x: 2, y: 2, z: 4, core: 2. Of those that a mesh axis runs over, the one named last changes fastest.
Arguments:
- ensemble: float32 [128, 3, 32, 1024], P('grp', None, 'gx', 'gy'), parts along dimension 0, may hold values from -16 to 16
- diffusivity: float32 [6, 32, 1024], P('grp', 'gx', 'gy'), parts along dimension 0, may hold values from 0.03 to 0.24
- mixing: float32 [3, 3], replicated, may hold values from -0.6 to 0.6
- obs_cell: int32 [4, 4, 4096], P('gx', 'gy', 'grp'), parts along dimension 2, may hold values from 0 to 2047
- obs_var: int32 [4, 4, 4096], P('gx', 'gy', 'grp'), parts along dimension 2, may hold values from 0 to 2
- obs_value: float32 [4, 4, 4096], P('gx', 'gy', 'grp'), parts along dimension 2, may hold values from -5 to 5
- obs_weight: float32 [4, 4, 4096], P('gx', 'gy', 'grp'), parts along dimension 2, may hold values from 0.5 to 6
Outputs:
- analysis: float32 [128, 3, 32, 1024], P('grp', None, 'gx', 'gy'), parts along dimension 0
There are 2 independent parts, one for each index of `grp`. A program takes and returns all parts, laid end to end along the dimension named above; an argument that names none is the same for every part. Nothing has to cross between parts.
All inputs are finite; a program needn't handle non-finite values.
Results may differ from a plain program's by a relative error of at most 0.0001.
Values sent between devices are 32-bit elements; how exact they have to be, the bound alone decides.
No kernel may reach another device: no remote copies, remote signals or barrier semaphores. Data moves between devices by JAX's collectives and lax.ppermute only.
A program may use at most 64 MiB of HBM per device.

v0:
```python
import math
import jax
import jax.numpy as jnp
from jax import lax
from jax.sharding import PartitionSpec as P

NS_ITERS = 5


def padded_2(cells, sides, width):
    for axis, dim in sides:
        count = lax.axis_size(axis)
        ends = count - 1
        head = lax.slice_in_dim(cells, 0, width, axis=dim)
        tail = lax.slice_in_dim(cells, cells.shape[dim] - width, cells.shape[dim], axis=dim)
        cells = jnp.concatenate(
            [
                lax.ppermute(tail, axis, [(i, (i + 1) % count) for i in range(ends)]),
                cells,
                lax.ppermute(head, axis, [((i + 1) % count, i) for i in range(ends)]),
            ],
            axis=dim,
        )
    return cells


def advance(padded, kappa_field, mixing):
    center = padded[:, :, 1:-1, 1:-1]
    beside = padded[:, :, 2:, 1:-1] + padded[:, :, :-2, 1:-1]
    beside = beside + padded[:, :, 1:-1, 2:] + padded[:, :, 1:-1, :-2]
    coupled = jnp.zeros_like(center)
    for source in range(3):
        coupled = coupled + mixing[:, source][None, :, None, None] * center[:, source][:, None]
    return center + kappa_field[None] * (beside - 4.0 * center) + coupled


def pad_faces(state):
    return padded_2(state, (("gx", 2), ("gy", 3)), 1)


def transform(gram, pull):
    identity = jnp.eye(gram.shape[0], dtype=jnp.float32)
    matrix = identity + gram
    frob_norm = jnp.sqrt(jnp.sum(matrix * matrix))

    def ns_step(step, carry):
        sqrt_iter, inv_iter = carry
        correction = 1.5 * identity - 0.5 * jnp.dot(
            inv_iter, sqrt_iter, precision=lax.Precision.HIGHEST
        )
        return (
            jnp.dot(sqrt_iter, correction, precision=lax.Precision.HIGHEST),
            jnp.dot(correction, inv_iter, precision=lax.Precision.HIGHEST),
        )

    sqrt_iter, inv_iter = lax.fori_loop(0, NS_ITERS, ns_step, (matrix / frob_norm, identity))
    root_inv = inv_iter / jnp.sqrt(frob_norm)
    inverse = jnp.dot(root_inv, root_inv, precision=lax.Precision.HIGHEST)
    mean_shift = jnp.dot(inverse, pull, precision=lax.Precision.HIGHEST)
    return mean_shift[:, None] + root_inv


def local(ensemble, diffusivity, mixing, obs_cell, obs_var, obs_value, obs_weight):
    members = ensemble.shape[0]
    first_state = advance(pad_faces(ensemble), diffusivity, mixing)
    second_state = advance(pad_faces(first_state), diffusivity, mixing)
    cell_count = second_state.shape[2] * second_state.shape[3]
    flat_state = second_state.reshape(members, -1)
    obs_index = obs_var[0, 0] * cell_count + obs_cell[0, 0]
    observed = jnp.take(flat_state, obs_index, axis=1)
    obs_mean = jnp.mean(observed, axis=0)
    obs_total = obs_cell.shape[2] * lax.axis_size("gx") * lax.axis_size("gy")
    factor = 1.0 / math.sqrt((members - 1) * obs_total)
    weight = obs_weight[0, 0]
    spread = (observed - obs_mean) * (weight * factor)
    departure = weight * (obs_value[0, 0] - obs_mean)
    gram_part = jnp.dot(spread, spread.T, precision=lax.Precision.HIGHEST)
    pull_part = jnp.dot(spread, departure, precision=lax.Precision.HIGHEST)
    gram, pull = lax.psum((gram_part, pull_part), ("gx", "gy"))
    state_mean = jnp.mean(second_state, axis=0)
    anomalies = (second_state - state_mean).reshape(members, -1)
    weights = transform(gram, pull)
    moved = jnp.dot(weights.T, anomalies, precision=lax.Precision.HIGHEST)
    return state_mean + moved.reshape(second_state.shape)


def solution(mesh):
    return jax.shard_map(
        local,
        mesh=mesh,
        in_specs=(
            P("grp", None, "gx", "gy"),
            P("grp", "gx", "gy"),
            P(),
            P("gx", "gy", "grp"),
            P("gx", "gy", "grp"),
            P("gx", "gy", "grp"),
            P("gx", "gy", "grp"),
        ),
        out_specs=P("grp", None, "gx", "gy"),
        check_vma=False,
    )
```

profile of v0, /device:TPU:2, one launch (start us, length us, event | category | flops | bytes accessed | tf_op | source)
XLA Modules:
  0.0 147.9 jit_solution(570074319774280910)
XLA Ops:
  0.0 2.0 %copy.48 = f32[64,3,8,256]{3,0,2,1:T(8,128)S(1)} copy(f32[64,3,8,256]{3,2,1,0:T(8,128)} %param.9) | data formatting | bytes 3145728 | tf_op args[0]
  2.1 1.9 %collective-permute-start.1 = (f32[64,3,1,256]{3,0,2,1:T(8,128)S(1)}, f32[64,3,1,256]{3,0,2,1:T(8,128)S(1)}, u32[]{:S(2)}, u32[]{:S(2)}) collective-permute-start(f32[64,3,1,256]{3,0,2,1:T(8,128)S(1)} %get-tuple-element.73), channel_id=1, source_target_pairs={{0,4},{4,8},{8,12},{1,5},{5,9},{9,13},{2,6},{6,10},{10,14},{3,7},{... | collective-permute-start | bytes 589832 | tf_op jit(solution)/shard_map/ppermute | solution.py:18
  4.0 3.6 %collective-permute-start = (f32[64,3,1,256]{3,0,2,1:T(8,128)S(1)}, f32[64,3,1,256]{3,0,2,1:T(8,128)S(1)}, u32[]{:S(2)}, u32[]{:S(2)}) collective-permute-start(f32[64,3,1,256]{3,0,2,1:T(8,128)S(1)} %get-tuple-element.72), channel_id=1, source_target_pairs={{4,0},{8,4},{12,8},{5,1},{9,5},{13,9},{6,2},{10,6},{14,10},{7,3},{... | collective-permute-start | bytes 589832 | tf_op jit(solution)/shard_map/ppermute | solution.py:20
  7.7 1.1 slice_bitcast_fusion.5
  8.8 0.6 fusion.34
  9.5 0.5 constant_dynamic-update-slice_fusion.1
  10.1 0.7 collective-permute-done
  10.9 1.3 fusion.44
  12.2 1.6 %copy.43 = f32[64,3,10,1]{0,3,2,1:T(1,128)S(1)} copy(f32[64,3,10,1]{3,0,2,1:T(8,128)} %get-tuple-element.62) | data formatting | bytes 15360 | tf_op jit(solution)/shard_map/slice | solution.py:14
  13.7 1.3 collective-permute-start.2
  15.0 0.3 copy.45
  15.4 4.6 %collective-permute-start.3 = (f32[64,3,10,1]{0,3,2,1:T(1,128)S(1)}, f32[64,3,10,1]{0,3,2,1:T(1,128)S(1)}, u32[]{:S(2)}, u32[]{:S(2)}) collective-permute-start(f32[64,3,10,1]{0,3,2,1:T(1,128)S(1)} %copy.45), channel_id=1, source_target_pairs={{0,1},{1,2},{2,3},{4,5},{5,6},{6,7},{8,9},{9,10},{10,11},{12,13},{... | collective-permute-start | bytes 23048 | tf_op jit(solution)/shard_map/ppermute | solution.py:18
  20.0 0.7 slice_reduce_fusion.2
  20.7 2.0 %copy.49 = f32[64,8,256]{2,0,1:T(8,128)} copy(f32[64,8,256]{2,1,0:T(8,128)} %get-tuple-element.69) | data formatting | bytes 1048576 | tf_op jit(solution)/shard_map/mul | solution.py:33
  22.7 2.0 %copy.50 = f32[64,8,256]{2,0,1:T(8,128)} copy(f32[64,8,256]{2,1,0:T(8,128)} %get-tuple-element.71) | data formatting | bytes 1048576 | tf_op jit(solution)/shard_map/mul | solution.py:33
  24.7 1.0 copy.51
  25.7 1.4 copy.44
  27.1 1.3 copy.46
  28.4 5.0 %fusion.14 = f32[64,3,8,256]{3,0,2,1:T(8,128)S(1)} fusion(f32[64,3,8,256]{3,0,2,1:T(8,128)} %copy-done.2, f32[64,3,10,256]{3,0,2,1:T(8,128)S(1)} %constant_dynamic-update-slice_fusion, f32[64,3,10,1]{3,0,2,1:T(8,128)} %copy.46, f32[64,3,10,1]{3,0,2,1:T(8,128)} %copy.44, f32[64,3,1,256]{3,0,2,1:T(8,128)} %copy-done.5, f32[64,3,1,256]{3,0,2,1:T(8,128)} %copy-done.6, ...), kind=kLoop, calls=%fused_computation.27 | loop fusion | flops 6684672 | bytes 7117860 | tf_op jit(solution)/shard_map/add | solution.py:34
  33.4 3.3 %collective-permute-start.4 = (f32[64,3,1,256]{3,0,2,1:T(8,128)S(1)}, f32[64,3,1,256]{3,0,2,1:T(8,128)S(1)}, u32[]{:S(2)}, u32[]{:S(2)}) collective-permute-start(f32[64,3,1,256]{3,0,2,1:T(8,128)S(1)} %get-tuple-element.65), channel_id=1, source_target_pairs={{4,0},{8,4},{12,8},{5,1},{9,5},{13,9},{6,2},{10,6},{14,10},{7,3},{... | collective-permute-start | bytes 589832 | tf_op jit(solution)/shard_map/ppermute | solution.py:20
  36.7 1.9 %collective-permute-start.5 = (f32[64,3,1,256]{3,0,2,1:T(8,128)S(1)}, f32[64,3,1,256]{3,0,2,1:T(8,128)S(1)}, u32[]{:S(2)}, u32[]{:S(2)}) collective-permute-start(f32[64,3,1,256]{3,0,2,1:T(8,128)S(1)} %get-tuple-element.64), channel_id=1, source_target_pairs={{0,4},{4,8},{8,12},{1,5},{5,9},{9,13},{2,6},{6,10},{10,14},{3,7},{... | collective-permute-start | bytes 589832 | tf_op jit(solution)/shard_map/ppermute | solution.py:18
  38.6 0.6 compare_and_fusion
  39.2 0.7 collective-permute-done.4
  39.9 3.8 %collective-permute-done.5 = f32[64,3,1,256]{3,0,2,1:T(8,128)S(1)} collective-permute-done((f32[64,3,1,256]{3,0,2,1:T(8,128)S(1)}, f32[64,3,1,256]{3,0,2,1:T(8,128)S(1)}, u32[]{:S(2)}, u32[]{:S(2)}) %collective-permute-start.5) | collective-permute-done | bytes 196640 | tf_op jit(solution)/shard_map/ppermute | solution.py:18
  43.8 0.5 copy-done.8
  44.3 0.4 fusion.43
  44.7 1.0 copy.52
  45.7 1.3 collective-permute-start.6
  47.0 0.3 copy.54
  47.3 5.2 %collective-permute-start.7 = (f32[64,3,10,1]{0,3,2,1:T(1,128)S(1)}, f32[64,3,10,1]{0,3,2,1:T(1,128)}, u32[]{:S(2)}, u32[]{:S(2)}) collective-permute-start(f32[64,3,10,1]{0,3,2,1:T(1,128)S(1)} %copy.54), channel_id=1, source_target_pairs={{0,1},{1,2},{2,3},{4,5},{5,6},{6,7},{8,9},{9,10},{10,11},{12,13},{... | collective-permute-start | bytes 23048 | tf_op jit(solution)/shard_map/ppermute | solution.py:18
  52.4 1.2 slice_bitcast_fusion.2
  53.7 0.4 copy.53
  54.0 1.1 copy.55
  55.2 4.6 %fusion.41 = (f32[3,8,256]{2,1,0:T(8,128)}, f32[64,3,8,256]{3,0,2,1:T(8,128)}) fusion(f32[64,8,256]{2,0,1:T(8,128)} %get-tuple-element.68, f32[3]{0:T(128)S(1)} %copy-done.17, f32[64,8,256]{2,0,1:T(8,128)} %get-tuple-element.67, f32[3]{0:T(128)} %get-tuple-element.47, f32[64,8,256]{2,0,1:T(8,128)} %get-tuple-element.66, f32[3]{0:T(128)S(1)} %copy-done.16, ...), kind=kLoop, calls=%fused_computation.85 | loop fusion | flops 8644608 | bytes 5176356 | tf_op jit(solution)/shard_map/reduce_sum | solution.py:80
  59.8 2.1 %copy.64 = f32[64,3,8,256]{0,3,2,1:T(8,128)S(1)} copy(f32[64,3,8,256]{3,0,2,1:T(8,128)} %get-tuple-element.59) | data formatting | bytes 3145728 | tf_op jit(solution)/shard_map/reshape | solution.py:68
  61.9 7.6 %gather_fusion = f32[2048,64]{1,0:T(8,128)} fusion(f32[64,6144]{0,1:T(8,128)S(1)} %bitcast.68, s32[2048]{0:T(1024)S(1)} %broadcast_clamp_fusion), kind=kCustom, calls=%fused_computation | custom fusion | bytes 1056768 | tf_op jit(solution)/shard_map/jit(_take)/gather | solution.py:70
  69.6 1.9 %select_reduce_fusion = f32[2048]{0:T(1024)S(1)} fusion(f32[2048,64]{1,0:T(8,128)} %gather_fusion, pred[2048]{0:T(1024)(128)(4,1)S(1)} %copy-done.11), kind=kLoop, calls=%fused_computation.40 | loop fusion | flops 260096 | bytes 534528 | tf_op jit(solution)/shard_map/reduce_sum | solution.py:71
  71.6 5.4 %fusion.23 = f32[64,64]{1,0:T(8,128)S(1)} fusion(f32[2048,64]{1,0:T(8,128)} %gather_fusion, f32[2048]{0:T(1024)S(1)} %get-tuple-element.76, f32[2048]{0:T(1024)S(1)} %get-tuple-element.75, pred[2048]{0:T(1024)(128)(4,1)S(1)} %copy-done.11), kind=kOutput, calls=%fused_computation.41 | convolution fusion | flops 101056512 | bytes 559104 | tf_op jit(solution)/shard_map/dot_general | solution.py:77
  77.0 1.3 convolution_bitcast_fusion.1
  78.3 59.5 %all-reduce = (f32[64,64]{1,0:T(8,128)S(1)}, f32[64]{0:T(128)S(1)}) all-reduce(f32[64,64]{1,0:T(8,128)S(1)} %fusion.23, f32[64]{0:T(128)S(1)} %convolution_bitcast_fusion.1), channel_id=1, replica_groups=mesh['grp'=2,'gx'=4,'gy'=4] {'gx','gy'}, use_global_device_ids=true, to_apply=%region_2.3 | all-reduce | flops 4160 | bytes 33280 | tf_op jit(solution)/shard_map/psum | solution.py:79
  137.9 0.6 multiply_reduce_fusion
  139.2 3.2 %while.13 = (s32[]{:T(128)}, f32[64,64]{0,1:T(8,128)S(1)}, f32[64,64]{1,0:T(8,128)S(1)}, s32[]{:T(128)}) while((s32[]{:T(128)}, f32[64,64]{0,1:T(8,128)S(1)}, f32[64,64]{1,0:T(8,128)S(1)}, s32[]{:T(128)}) %tuple.41), condition=%wide.region_5.6_spmd.clone, body=%wide.region_4.5_spmd.clone.sunk | while | flops 9453570 | bytes 213045 | solution.py:56
  139.6 0.2 convolution_bitcast_fusion.4
  140.3 0.2 convolution_bitcast_fusion.4
  140.9 0.2 convolution_bitcast_fusion.4
  142.6 0.9 copy.68
  143.9 2.0 %fusion.19 = f32[64,3,8,256]{3,0,2,1:T(8,128)S(1)} fusion(f32[3,8,256,64]{2,1,0,3:T(8,128)S(1)} %bitcast.69, f32[3,8,256]{2,1,0:T(8,128)S(1)} %broadcast_multiply_fusion, f32[64]{0:T(128)S(1)} %convolution_bitcast_fusion.2, f32[64,64]{1,0:T(8,128)S(1)} %get-tuple-element.27, f32[]{:T(128)S(6)} %sqrt.7), kind=kOutput, calls=%fused_computation.35 | convolution fusion | flops 302391296 | bytes 3186948 | tf_op jit(solution)/shard_map/dot_general | solution.py:83
  145.8 2.1 %copy.62 = f32[64,3,8,256]{3,2,1,0:T(8,128)} copy(f32[64,3,8,256]{3,0,2,1:T(8,128)S(1)} %fusion.19) | data formatting | bytes 3145728 | tf_op jit(solution)/shard_map/add | solution.py:84
  (76 shorter events, 3.3 us)
Async XLA Ops:
  0.0 7.7 %copy-start = (f32[64,3,8,256]{3,2,1,0:T(8,128)S(1)}, f32[64,3,8,256]{3,2,1,0:T(8,128)}, u32[]{:S(2)}) copy-start(f32[64,3,8,256]{3,2,1,0:T(8,128)} %param.9) | copy-start | bytes 4718596
  2.0 6.8 %copy-start.2 = (f32[64,3,8,256]{3,0,2,1:T(8,128)}, f32[64,3,8,256]{3,0,2,1:T(8,128)S(1)}, u32[]{:S(2)}) copy-start(f32[64,3,8,256]{3,0,2,1:T(8,128)S(1)} %copy.48) | copy-start | bytes 4718596
  2.1 7.4 %collective-permute-start.1 = (f32[64,3,1,256]{3,0,2,1:T(8,128)S(1)}, f32[64,3,1,256]{3,0,2,1:T(8,128)S(1)}, u32[]{:S(2)}, u32[]{:S(2)}) collective-permute-start(f32[64,3,1,256]{3,0,2,1:T(8,128)S(1)} %get-tuple-element.73), channel_id=1, source_target_pairs={{0,4},{4,8},{8,12},{1,5},{5,9},{9,13},{2,6},{6,10},{10,14},{3,7},{... | collective-permute-start | bytes 589832 | tf_op jit(solution)/shard_map/ppermute | solution.py:18
  4.0 5.4 %copy-start.12 = (s32[1,1,2048]{2,1,0:T(1,128)S(1)}, s32[1,1,2048]{2,1,0:T(1,128)}, u32[]{:S(2)}) copy-start(s32[1,1,2048]{2,1,0:T(1,128)} %param.12) | copy-start | bytes 24580
  4.0 5.4 %copy-start.13 = (s32[1,1,2048]{2,1,0:T(1,128)S(1)}, s32[1,1,2048]{2,1,0:T(1,128)}, u32[]{:S(2)}) copy-start(s32[1,1,2048]{2,1,0:T(1,128)} %param.13) | copy-start | bytes 24580
  4.0 6.8 %collective-permute-start = (f32[64,3,1,256]{3,0,2,1:T(8,128)S(1)}, f32[64,3,1,256]{3,0,2,1:T(8,128)S(1)}, u32[]{:S(2)}, u32[]{:S(2)}) collective-permute-start(f32[64,3,1,256]{3,0,2,1:T(8,128)S(1)} %get-tuple-element.72), channel_id=1, source_target_pairs={{4,0},{8,4},{12,8},{5,1},{9,5},{13,9},{6,2},{10,6},{14,10},{7,3},{... | collective-permute-start | bytes 589832 | tf_op jit(solution)/shard_map/ppermute | solution.py:20
  9.5 0.7 copy-start.5
  10.9 1.3 copy-start.6
  12.2 7.8 %copy-start.10 = (f32[3,3]{1,0:T(4,128)S(1)}, f32[3,3]{1,0:T(4,128)}, u32[]{:S(2)}) copy-start(f32[3,3]{1,0:T(4,128)} %param.11) | copy-start | bytes 112
  13.7 12.0 %collective-permute-start.2 = (f32[64,3,10,1]{0,3,2,1:T(1,128)S(1)}, f32[64,3,10,1]{0,3,2,1:T(1,128)S(1)}, u32[]{:S(2)}, u32[]{:S(2)}) collective-permute-start(f32[64,3,10,1]{0,3,2,1:T(1,128)S(1)} %copy.43), channel_id=1, source_target_pairs={{1,0},{2,1},{3,2},{5,4},{6,5},{7,6},{9,8},{10,9},{11,10},{13,12},{... | collective-permute-start | bytes 23048 | tf_op jit(solution)/shard_map/ppermute | solution.py:20
  15.4 11.7 %collective-permute-start.3 = (f32[64,3,10,1]{0,3,2,1:T(1,128)S(1)}, f32[64,3,10,1]{0,3,2,1:T(1,128)S(1)}, u32[]{:S(2)}, u32[]{:S(2)}) collective-permute-start(f32[64,3,10,1]{0,3,2,1:T(1,128)S(1)} %copy.45), channel_id=1, source_target_pairs={{0,1},{1,2},{2,3},{4,5},{5,6},{6,7},{8,9},{9,10},{10,11},{12,13},{... | collective-permute-start | bytes 23048 | tf_op jit(solution)/shard_map/ppermute | solution.py:18
  33.4 6.4 %collective-permute-start.4 = (f32[64,3,1,256]{3,0,2,1:T(8,128)S(1)}, f32[64,3,1,256]{3,0,2,1:T(8,128)S(1)}, u32[]{:S(2)}, u32[]{:S(2)}) collective-permute-start(f32[64,3,1,256]{3,0,2,1:T(8,128)S(1)} %get-tuple-element.65), channel_id=1, source_target_pairs={{4,0},{8,4},{12,8},{5,1},{9,5},{13,9},{6,2},{10,6},{14,10},{7,3},{... | collective-permute-start | bytes 589832 | tf_op jit(solution)/shard_map/ppermute | solution.py:20
  36.7 7.0 %collective-permute-start.5 = (f32[64,3,1,256]{3,0,2,1:T(8,128)S(1)}, f32[64,3,1,256]{3,0,2,1:T(8,128)S(1)}, u32[]{:S(2)}, u32[]{:S(2)}) collective-permute-start(f32[64,3,1,256]{3,0,2,1:T(8,128)S(1)} %get-tuple-element.64), channel_id=1, source_target_pairs={{0,4},{4,8},{8,12},{1,5},{5,9},{9,13},{2,6},{6,10},{10,14},{3,7},{... | collective-permute-start | bytes 589832 | tf_op jit(solution)/shard_map/ppermute | solution.py:18
  39.9 4.0 %copy-start.7 = (f32[64,3,1,256]{3,0,2,1:T(8,128)}, f32[64,3,1,256]{3,0,2,1:T(8,128)S(1)}, u32[]{:S(2)}) copy-start(f32[64,3,1,256]{3,0,2,1:T(8,128)S(1)} %collective-permute-done.4) | copy-start | bytes 589828
  43.7 0.7 copy-start.8
  45.7 8.0 %collective-permute-start.6 = (f32[64,3,10,1]{0,3,2,1:T(1,128)}, f32[64,3,10,1]{0,3,2,1:T(1,128)S(1)}, u32[]{:S(2)}, u32[]{:S(2)}) collective-permute-start(f32[64,3,10,1]{0,3,2,1:T(1,128)} %copy.52), channel_id=1, source_target_pairs={{1,0},{2,1},{3,2},{5,4},{6,5},{7,6},{9,8},{10,9},{11,10},{13,12},{... | collective-permute-start | bytes 23048 | tf_op jit(solution)/shard_map/ppermute | solution.py:20
  47.3 6.7 %collective-permute-start.7 = (f32[64,3,10,1]{0,3,2,1:T(1,128)S(1)}, f32[64,3,10,1]{0,3,2,1:T(1,128)}, u32[]{:S(2)}, u32[]{:S(2)}) collective-permute-start(f32[64,3,10,1]{0,3,2,1:T(1,128)S(1)} %copy.54), channel_id=1, source_target_pairs={{0,1},{1,2},{2,3},{4,5},{5,6},{6,7},{8,9},{9,10},{10,11},{12,13},{... | collective-permute-start | bytes 23048 | tf_op jit(solution)/shard_map/ppermute | solution.py:18
  53.6 1.5 %copy-start.16 = (f32[3]{0:T(128)S(1)}, f32[3]{0:T(128)}, u32[]{:S(2)}) copy-start(f32[3]{0:T(128)} %get-tuple-element.45) | copy-start | bytes 40
  53.6 1.5 %copy-start.17 = (f32[3]{0:T(128)S(1)}, f32[3]{0:T(128)}, u32[]{:S(2)}) copy-start(f32[3]{0:T(128)} %get-tuple-element.46) | copy-start | bytes 40
  61.9 7.7 %copy-start.11 = (pred[2048]{0:T(1024)(128)(4,1)S(1)}, pred[2048]{0:T(1024)(128)(4,1)}, u32[]{:S(2)}) copy-start(pred[2048]{0:T(1024)(128)(4,1)} %compare_and_fusion) | copy-start | bytes 6148
  61.9 9.6 %copy-start.14 = (f32[1,1,2048]{2,1,0:T(1,128)S(1)}, f32[1,1,2048]{2,1,0:T(1,128)}, u32[]{:S(2)}) copy-start(f32[1,1,2048]{2,1,0:T(1,128)} %param.15) | copy-start | bytes 24580
  61.9 9.6 %copy-start.15 = (f32[1,1,2048]{2,1,0:T(1,128)S(1)}, f32[1,1,2048]{2,1,0:T(1,128)}, u32[]{:S(2)}) copy-start(f32[1,1,2048]{2,1,0:T(1,128)} %param.14) | copy-start | bytes 24580
  69.6 7.4 %copy-start.3 = (f32[2048,64]{1,0:T(8,128)S(1)}, f32[2048,64]{1,0:T(8,128)}, u32[]{:S(2)}) copy-start(f32[2048,64]{1,0:T(8,128)} %gather_fusion) | copy-start | bytes 1572868
  69.6 69.6 %copy-start.4 = (f32[64,64]{1,0:T(8,128)S(1)}, f32[64,64]{1,0:T(8,128)}, u32[]{:S(2)}) copy-start(f32[64,64]{1,0:T(8,128)} %fusion.34) | copy-start | bytes 49156
  77.0 65.5 %copy-start.9 = (f32[3,8,256]{2,1,0:T(8,128)S(1)}, f32[3,8,256]{2,1,0:T(8,128)}, u32[]{:S(2)}) copy-start(f32[3,8,256]{2,1,0:T(8,128)} %get-tuple-element.58) | copy-start | bytes 73732
  77.0 65.5 %copy-start.1 = (f32[64,3,8,256]{3,0,2,1:T(8,128)S(1)}, f32[64,3,8,256]{3,0,2,1:T(8,128)}, u32[]{:S(2)}) copy-start(f32[64,3,8,256]{3,0,2,1:T(8,128)} %get-tuple-element.59) | copy-start | bytes 4718596
where the time goes:
time: 148 us
  blocking collectives  59.5 us (40%)
  local copies, waits for them, and re-layouts  33.2 us (22%)
  starting transfers between devices  23 us (16%)
  other arithmetic  13.7 us (9%)
  matrix products  11.9 us (8%)
  waiting for transfers between devices  5.19 us (4%)
    psum x1, blocking collectives, local(): gram, pull = lax.psum((gram_part, pull_part), ('gx', 'gy'))  59.5 us
    ppermute x4, starting transfers between devices, padded_2(): lax.ppermute(tail, axis, [(i, (i + 1) % count) for i in range(ends)])  13.5 us
    ppermute x4, starting transfers between devices, padded_2(): lax.ppermute(head, axis, [((i + 1) % count, i) for i in range(ends)])  9.47 us
    gather x1, local copies, waits for them, and re-layouts, local(): observed = jnp.take(flat_state, obs_index, axis=1)  7.62 us
    mul x5, local copies, waits for them, and re-layouts, advance(): mixing[:, source][None, :, None, None] * center[:, source][:, None]  7.33 us
    dot_general x1, matrix products, local(): gram_part = jnp.dot(spread, spread.T, precision=lax.Precision.HIGHEST)  5.4 us
    add x1, other arithmetic, advance(): return center + kappa_field[None] * (beside - 4.0 * center) + coupled  4.97 us
    reduce_sum x1, other arithmetic, local(): state_mean = jnp.mean(second_state, axis=0)  4.63 us
  transfers between devices with their start and end apart: 8, of which 3 were waited for; matrix products, arithmetic and copies ran while one was open for 8% of the time, Pallas kernels for 0%

commit v1 on v0

--- a/solution.py
+++ b/solution.py
@@ -76,7 +76,13 @@
     departure = weight * (obs_value[0, 0] - obs_mean)
     gram_part = jnp.dot(spread, spread.T, precision=lax.Precision.HIGHEST)
     pull_part = jnp.dot(spread, departure, precision=lax.Precision.HIGHEST)
-    gram, pull = lax.psum((gram_part, pull_part), ("gx", "gy"))
+
+    def rings_compute(sample, device_axis, mesh_name):
+        res = lax.psum(sample, device_axis)
+        top = lax.psum(res, mesh_name)
+        return top
+
+    gram, pull = rings_compute((gram_part, pull_part), "gy", "gx")
     state_mean = jnp.mean(second_state, axis=0)
     anomalies = (second_state - state_mean).reshape(members, -1)
     weights = transform(gram, pull)

time: 148 us -> 120 us (0.81)
  blocking collectives: 59.5 us -> 30.3 us
    psum x1 -> x2, blocking collectives: 59.5 us -> 30.3 us  [the longest x1 19.6 us: rings_compute(): res = lax.psum(sample, device_axis)]
  transfers between devices with their start and end apart: 8 -> 8, of which waited for: 3 -> 3; matrix products, arithmetic and copies ran while one was open for 8% -> 10% of each run, Pallas kernels for 0% -> 0%
where the time goes in v1:
time: 120 us; the launch traced here: 119 us
  local copies, waits for them, and re-layouts  33.3 us (28%)
  blocking collectives  30.3 us (25%)
  starting transfers between devices  23 us (19%)
  other arithmetic  13.7 us (11%)
  matrix products  11.9 us (10%)
  waiting for transfers between devices  5.23 us (4%)
  between operations  1.21 us (1%)
    psum x1, blocking collectives, rings_compute(): res = lax.psum(sample, device_axis)  19.6 us
    ppermute x4, starting transfers between devices, padded_2(): lax.ppermute(tail, axis, [(i, (i + 1) % count) for i in range(ends)])  13.5 us
    psum x1, blocking collectives, rings_compute(): top = lax.psum(res, mesh_name)  10.7 us
    ppermute x4, starting transfers between devices, padded_2(): lax.ppermute(head, axis, [((i + 1) % count, i) for i in range(ends)])  9.47 us
    gather x1, local copies, waits for them, and re-layouts, local(): observed = jnp.take(flat_state, obs_index, axis=1)  7.61 us
    mul x5, local copies, waits for them, and re-layouts, advance(): mixing[:, source][None, :, None, None] * center[:, source][:, None]  7.33 us
    dot_general x1, matrix products, local(): gram_part = jnp.dot(spread, spread.T, precision=lax.Precision.HIGHEST)  5.4 us
    add x1, other arithmetic, advance(): return center + kappa_field[None] * (beside - 4.0 * center) + coupled  4.94 us
  transfers between devices with their start and end apart: 8, of which 3 were waited for; matrix products, arithmetic and copies ran while one was open for 10% of the time, Pallas kernels for 0%

profile of v1, /device:TPU:2, one launch (start us, length us, event | category | flops | bytes accessed | tf_op | source)
XLA Modules:
  0.0 118.9 jit_solution(3716605879104398254)
XLA Ops:
  0.0 2.0 %copy.48 = f32[64,3,8,256]{3,0,2,1:T(8,128)S(1)} copy(f32[64,3,8,256]{3,2,1,0:T(8,128)} %param.9) | data formatting | bytes 3145728 | tf_op args[0]
  2.1 1.9 %collective-permute-start.1 = (f32[64,3,1,256]{3,0,2,1:T(8,128)S(1)}, f32[64,3,1,256]{3,0,2,1:T(8,128)S(1)}, u32[]{:S(2)}, u32[]{:S(2)}) collective-permute-start(f32[64,3,1,256]{3,0,2,1:T(8,128)S(1)} %get-tuple-element.75), channel_id=1, source_target_pairs={{0,4},{4,8},{8,12},{1,5},{5,9},{9,13},{2,6},{6,10},{10,14},{3,7},{... | collective-permute-start | bytes 589832 | tf_op jit(solution)/shard_map/ppermute | solution.py:18
  4.0 3.6 %collective-permute-start = (f32[64,3,1,256]{3,0,2,1:T(8,128)S(1)}, f32[64,3,1,256]{3,0,2,1:T(8,128)S(1)}, u32[]{:S(2)}, u32[]{:S(2)}) collective-permute-start(f32[64,3,1,256]{3,0,2,1:T(8,128)S(1)} %get-tuple-element.74), channel_id=1, source_target_pairs={{4,0},{8,4},{12,8},{5,1},{9,5},{13,9},{6,2},{10,6},{14,10},{7,3},{... | collective-permute-start | bytes 589832 | tf_op jit(solution)/shard_map/ppermute | solution.py:20
  7.7 1.1 slice_bitcast_fusion.5
  8.8 0.6 fusion.34
  9.5 0.5 constant_dynamic-update-slice_fusion.1
  10.1 0.7 collective-permute-done
  10.9 1.3 %fusion.44 = (f32[64,3,10,1]{3,0,2,1:T(8,128)}, f32[64,3,10,1]{3,0,2,1:T(8,128)S(1)}) fusion(f32[64,3,10,256]{3,0,2,1:T(8,128)S(1)} %constant_dynamic-update-slice_fusion), kind=kLoop, calls=%fused_computation.87 | loop fusion | bytes 30720 | tf_op jit(solution)/shard_map/slice | solution.py:14
  12.2 1.6 %copy.43 = f32[64,3,10,1]{0,3,2,1:T(1,128)S(1)} copy(f32[64,3,10,1]{3,0,2,1:T(8,128)} %get-tuple-element.64) | data formatting | bytes 15360 | tf_op jit(solution)/shard_map/slice | solution.py:14
  13.7 1.3 %collective-permute-start.2 = (f32[64,3,10,1]{0,3,2,1:T(1,128)S(1)}, f32[64,3,10,1]{0,3,2,1:T(1,128)S(1)}, u32[]{:S(2)}, u32[]{:S(2)}) collective-permute-start(f32[64,3,10,1]{0,3,2,1:T(1,128)S(1)} %copy.43), channel_id=1, source_target_pairs={{1,0},{2,1},{3,2},{5,4},{6,5},{7,6},{9,8},{10,9},{11,10},{13,12},{... | collective-permute-start | bytes 23048 | tf_op jit(solution)/shard_map/ppermute | solution.py:20
  15.0 0.3 copy.45
  15.4 4.6 %collective-permute-start.3 = (f32[64,3,10,1]{0,3,2,1:T(1,128)S(1)}, f32[64,3,10,1]{0,3,2,1:T(1,128)S(1)}, u32[]{:S(2)}, u32[]{:S(2)}) collective-permute-start(f32[64,3,10,1]{0,3,2,1:T(1,128)S(1)} %copy.45), channel_id=1, source_target_pairs={{0,1},{1,2},{2,3},{4,5},{5,6},{6,7},{8,9},{9,10},{10,11},{12,13},{... | collective-permute-start | bytes 23048 | tf_op jit(solution)/shard_map/ppermute | solution.py:18
  19.9 0.8 slice_reduce_fusion.2
  20.7 2.0 %copy.49 = f32[64,8,256]{2,0,1:T(8,128)} copy(f32[64,8,256]{2,1,0:T(8,128)} %get-tuple-element.71) | data formatting | bytes 1048576 | tf_op jit(solution)/shard_map/mul | solution.py:33
  22.7 2.0 %copy.50 = f32[64,8,256]{2,0,1:T(8,128)} copy(f32[64,8,256]{2,1,0:T(8,128)} %get-tuple-element.73) | data formatting | bytes 1048576 | tf_op jit(solution)/shard_map/mul | solution.py:33
  24.8 1.0 copy.51
  25.7 1.3 %copy.44 = f32[64,3,10,1]{3,0,2,1:T(8,128)} copy(f32[64,3,10,1]{0,3,2,1:T(1,128)S(1)} %collective-permute-done.2) | data formatting | bytes 15360 | tf_op jit(solution)/shard_map/ppermute | solution.py:20
  27.1 1.3 %copy.46 = f32[64,3,10,1]{3,0,2,1:T(8,128)} copy(f32[64,3,10,1]{0,3,2,1:T(1,128)S(1)} %collective-permute-done.3) | data formatting | bytes 15360 | tf_op jit(solution)/shard_map/ppermute | solution.py:18
  28.4 4.9 %fusion.14 = f32[64,3,8,256]{3,0,2,1:T(8,128)S(1)} fusion(f32[64,3,8,256]{3,0,2,1:T(8,128)} %copy-done.2, f32[64,3,10,256]{3,0,2,1:T(8,128)S(1)} %constant_dynamic-update-slice_fusion, f32[64,3,10,1]{3,0,2,1:T(8,128)} %copy.46, f32[64,3,10,1]{3,0,2,1:T(8,128)} %copy.44, f32[64,3,1,256]{3,0,2,1:T(8,128)} %copy-done.5, f32[64,3,1,256]{3,0,2,1:T(8,128)} %copy-done.6, ...), kind=kLoop, calls=%fused_computation.27 | loop fusion | flops 6684672 | bytes 7117860 | tf_op jit(solution)/shard_map/add | solution.py:34
  33.4 3.3 %collective-permute-start.4 = (f32[64,3,1,256]{3,0,2,1:T(8,128)S(1)}, f32[64,3,1,256]{3,0,2,1:T(8,128)S(1)}, u32[]{:S(2)}, u32[]{:S(2)}) collective-permute-start(f32[64,3,1,256]{3,0,2,1:T(8,128)S(1)} %get-tuple-element.67), channel_id=1, source_target_pairs={{4,0},{8,4},{12,8},{5,1},{9,5},{13,9},{6,2},{10,6},{14,10},{7,3},{... | collective-permute-start | bytes 589832 | tf_op jit(solution)/shard_map/ppermute | solution.py:20
  36.7 1.9 %collective-permute-start.5 = (f32[64,3,1,256]{3,0,2,1:T(8,128)S(1)}, f32[64,3,1,256]{3,0,2,1:T(8,128)S(1)}, u32[]{:S(2)}, u32[]{:S(2)}) collective-permute-start(f32[64,3,1,256]{3,0,2,1:T(8,128)S(1)} %get-tuple-element.66), channel_id=1, source_target_pairs={{0,4},{4,8},{8,12},{1,5},{5,9},{9,13},{2,6},{6,10},{10,14},{3,7},{... | collective-permute-start | bytes 589832 | tf_op jit(solution)/shard_map/ppermute | solution.py:18
  38.6 0.6 compare_and_fusion
  39.2 0.7 collective-permute-done.4
  39.8 3.8 %collective-permute-done.5 = f32[64,3,1,256]{3,0,2,1:T(8,128)S(1)} collective-permute-done((f32[64,3,1,256]{3,0,2,1:T(8,128)S(1)}, f32[64,3,1,256]{3,0,2,1:T(8,128)S(1)}, u32[]{:S(2)}, u32[]{:S(2)}) %collective-permute-start.5) | collective-permute-done | bytes 196640 | tf_op jit(solution)/shard_map/ppermute | solution.py:18
  43.8 0.5 copy-done.8
  44.3 0.4 fusion.43
  44.7 1.0 copy.52
  45.7 1.3 %collective-permute-start.6 = (f32[64,3,10,1]{0,3,2,1:T(1,128)}, f32[64,3,10,1]{0,3,2,1:T(1,128)S(1)}, u32[]{:S(2)}, u32[]{:S(2)}) collective-permute-start(f32[64,3,10,1]{0,3,2,1:T(1,128)} %copy.52), channel_id=1, source_target_pairs={{1,0},{2,1},{3,2},{5,4},{6,5},{7,6},{9,8},{10,9},{11,10},{13,12},{... | collective-permute-start | bytes 23048 | tf_op jit(solution)/shard_map/ppermute | solution.py:20
  46.9 0.3 copy.54
  47.3 5.1 %collective-permute-start.7 = (f32[64,3,10,1]{0,3,2,1:T(1,128)S(1)}, f32[64,3,10,1]{0,3,2,1:T(1,128)}, u32[]{:S(2)}, u32[]{:S(2)}) collective-permute-start(f32[64,3,10,1]{0,3,2,1:T(1,128)S(1)} %copy.54), channel_id=1, source_target_pairs={{0,1},{1,2},{2,3},{4,5},{5,6},{6,7},{8,9},{9,10},{10,11},{12,13},{... | collective-permute-start | bytes 23048 | tf_op jit(solution)/shard_map/ppermute | solution.py:18
  52.4 1.2 %slice_bitcast_fusion.2 = (f32[64,8,256]{2,0,1:T(8,128)}, f32[64,8,256]{2,0,1:T(8,128)}, f32[64,8,256]{2,0,1:T(8,128)}) fusion(f32[64,3,8,256]{3,0,2,1:T(8,128)S(1)} %fusion.14), kind=kLoop, calls=%fused_computation.45 | loop fusion | bytes 3145728 | tf_op jit(solution)/shard_map/mul | solution.py:33
  53.7 0.4 copy.53
  54.1 1.1 copy.55
  55.2 4.6 %fusion.41 = (f32[3,8,256]{2,1,0:T(8,128)}, f32[64,3,8,256]{3,0,2,1:T(8,128)}) fusion(f32[64,8,256]{2,0,1:T(8,128)} %get-tuple-element.70, f32[3]{0:T(128)S(1)} %copy-done.17, f32[64,8,256]{2,0,1:T(8,128)} %get-tuple-element.69, f32[3]{0:T(128)} %get-tuple-element.47, f32[64,8,256]{2,0,1:T(8,128)} %get-tuple-element.68, f32[3]{0:T(128)S(1)} %copy-done.16, ...), kind=kLoop, calls=%fused_computation.85 | loop fusion | flops 8644608 | bytes 5176356 | tf_op jit(solution)/shard_map/reduce_sum | solution.py:86
  59.8 2.1 %copy.64 = f32[64,3,8,256]{0,3,2,1:T(8,128)S(1)} copy(f32[64,3,8,256]{3,0,2,1:T(8,128)} %get-tuple-element.61) | data formatting | bytes 3145728 | tf_op jit(solution)/shard_map/reshape | solution.py:68
  62.0 7.6 %gather_fusion = f32[2048,64]{1,0:T(8,128)} fusion(f32[64,6144]{0,1:T(8,128)S(1)} %bitcast.68, s32[2048]{0:T(1024)S(1)} %broadcast_clamp_fusion), kind=kCustom, calls=%fused_computation | custom fusion | bytes 1056768 | tf_op jit(solution)/shard_map/jit(_take)/gather | solution.py:70
  69.6 1.9 %select_reduce_fusion = f32[2048]{0:T(1024)S(1)} fusion(f32[2048,64]{1,0:T(8,128)} %gather_fusion, pred[2048]{0:T(1024)(128)(4,1)S(1)} %copy-done.11), kind=kLoop, calls=%fused_computation.40 | loop fusion | flops 260096 | bytes 534528 | tf_op jit(solution)/shard_map/reduce_sum | solution.py:71
  71.6 5.4 %fusion.23 = f32[64,64]{1,0:T(8,128)S(1)} fusion(f32[2048,64]{1,0:T(8,128)} %gather_fusion, f32[2048]{0:T(1024)S(1)} %get-tuple-element.78, f32[2048]{0:T(1024)S(1)} %get-tuple-element.77, pred[2048]{0:T(1024)(128)(4,1)S(1)} %copy-done.11), kind=kOutput, calls=%fused_computation.41 | convolution fusion | flops 101056512 | bytes 559104 | tf_op jit(solution)/shard_map/dot_general | solution.py:77
  77.0 1.3 %convolution_bitcast_fusion.1 = f32[64]{0:T(128)S(1)} fusion(f32[2048,1]{0,1:T(1,128)S(1)} %bitcast.75, f32[2048,64]{1,0:T(8,128)S(1)} %copy-done.3, f32[2048]{0:T(1024)S(1)} %get-tuple-element.78, f32[2048]{0:T(1024)S(1)} %get-tuple-element.77, pred[2048]{0:T(1024)(128)(4,1)S(1)} %copy-done.11), kind=kOutput, calls=%fused_computation.36 | convolution fusion | flops 1966080 | bytes 551168 | tf_op jit(solution)/shard_map/dot_general | solution.py:78
  78.3 19.6 %all-reduce = (f32[64,64]{1,0:T(8,128)S(1)}, f32[64]{0:T(128)S(1)}) all-reduce(f32[64,64]{1,0:T(8,128)S(1)} %fusion.23, f32[64]{0:T(128)S(1)} %convolution_bitcast_fusion.1), channel_id=1, replica_groups=mesh['grp'=2,'gx'=4,'gy'=4] {'gy'}, use_global_device_ids=true, to_apply=%region_2.3 | all-reduce | flops 4160 | bytes 33280 | tf_op jit(solution)/shard_map/psum | solution.py:81
  98.0 10.7 %all-reduce.1 = (f32[64,64]{1,0:T(8,128)S(1)}, f32[64]{0:T(128)S(1)}) all-reduce(f32[64,64]{1,0:T(8,128)S(1)} %get-tuple-element.54, f32[64]{0:T(128)S(1)} %get-tuple-element.55), channel_id=1, replica_groups=mesh['grp'=2,'gx'=4,'gy'=4] {'gx'}, use_global_device_ids=true, to_apply=%region_3.4 | all-reduce | flops 4160 | bytes 33280 | tf_op jit(solution)/shard_map/psum | solution.py:82
  108.6 0.7 multiply_reduce_fusion
  110.2 3.2 %while.13 = (s32[]{:T(128)}, f32[64,64]{0,1:T(8,128)S(1)}, f32[64,64]{1,0:T(8,128)S(1)}, s32[]{:T(128)}) while((s32[]{:T(128)}, f32[64,64]{0,1:T(8,128)S(1)}, f32[64,64]{1,0:T(8,128)S(1)}, s32[]{:T(128)}) %tuple.41), condition=%wide.region_6.7_spmd.clone, body=%wide.region_5.6_spmd.clone.sunk | while | flops 9453570 | bytes 213045 | solution.py:56
  110.6 0.2 convolution_bitcast_fusion.4
  111.2 0.2 convolution_bitcast_fusion.4
  113.6 0.9 copy.68
  114.8 1.9 %fusion.19 = f32[64,3,8,256]{3,0,2,1:T(8,128)S(1)} fusion(f32[3,8,256,64]{2,1,0,3:T(8,128)S(1)} %bitcast.69, f32[3,8,256]{2,1,0:T(8,128)S(1)} %broadcast_multiply_fusion, f32[64]{0:T(128)S(1)} %convolution_bitcast_fusion.2, f32[64,64]{1,0:T(8,128)S(1)} %get-tuple-element.27, f32[]{:T(128)S(6)} %sqrt.7), kind=kOutput, calls=%fused_computation.35 | convolution fusion | flops 302391296 | bytes 3186948 | tf_op jit(solution)/shard_map/dot_general | solution.py:89
  116.8 2.1 %copy.62 = f32[64,3,8,256]{3,2,1,0:T(8,128)} copy(f32[64,3,8,256]{3,0,2,1:T(8,128)S(1)} %fusion.19) | data formatting | bytes 3145728 | tf_op jit(solution)/shard_map/add | solution.py:90
  (77 shorter events, 3.5 us)
Async XLA Ops:
  0.0 7.7 %copy-start = (f32[64,3,8,256]{3,2,1,0:T(8,128)S(1)}, f32[64,3,8,256]{3,2,1,0:T(8,128)}, u32[]{:S(2)}) copy-start(f32[64,3,8,256]{3,2,1,0:T(8,128)} %param.9) | copy-start | bytes 4718596
  2.0 6.8 %copy-start.2 = (f32[64,3,8,256]{3,0,2,1:T(8,128)}, f32[64,3,8,256]{3,0,2,1:T(8,128)S(1)}, u32[]{:S(2)}) copy-start(f32[64,3,8,256]{3,0,2,1:T(8,128)S(1)} %copy.48) | copy-start | bytes 4718596
  2.1 7.4 %collective-permute-start.1 = (f32[64,3,1,256]{3,0,2,1:T(8,128)S(1)}, f32[64,3,1,256]{3,0,2,1:T(8,128)S(1)}, u32[]{:S(2)}, u32[]{:S(2)}) collective-permute-start(f32[64,3,1,256]{3,0,2,1:T(8,128)S(1)} %get-tuple-element.75), channel_id=1, source_target_pairs={{0,4},{4,8},{8,12},{1,5},{5,9},{9,13},{2,6},{6,10},{10,14},{3,7},{... | collective-permute-start | bytes 589832 | tf_op jit(solution)/shard_map/ppermute | solution.py:18
  4.0 5.4 %copy-start.12 = (s32[1,1,2048]{2,1,0:T(1,128)S(1)}, s32[1,1,2048]{2,1,0:T(1,128)}, u32[]{:S(2)}) copy-start(s32[1,1,2048]{2,1,0:T(1,128)} %param.12) | copy-start | bytes 24580
  4.0 5.4 %copy-start.13 = (s32[1,1,2048]{2,1,0:T(1,128)S(1)}, s32[1,1,2048]{2,1,0:T(1,128)}, u32[]{:S(2)}) copy-start(s32[1,1,2048]{2,1,0:T(1,128)} %param.13) | copy-start | bytes 24580
  4.0 6.8 %collective-permute-start = (f32[64,3,1,256]{3,0,2,1:T(8,128)S(1)}, f32[64,3,1,256]{3,0,2,1:T(8,128)S(1)}, u32[]{:S(2)}, u32[]{:S(2)}) collective-permute-start(f32[64,3,1,256]{3,0,2,1:T(8,128)S(1)} %get-tuple-element.74), channel_id=1, source_target_pairs={{4,0},{8,4},{12,8},{5,1},{9,5},{13,9},{6,2},{10,6},{14,10},{7,3},{... | collective-permute-start | bytes 589832 | tf_op jit(solution)/shard_map/ppermute | solution.py:20
  9.5 0.7 copy-start.5
  10.9 1.3 %copy-start.6 = (f32[64,3,1,256]{3,0,2,1:T(8,128)}, f32[64,3,1,256]{3,0,2,1:T(8,128)S(1)}, u32[]{:S(2)}) copy-start(f32[64,3,1,256]{3,0,2,1:T(8,128)S(1)} %collective-permute-done) | copy-start | bytes 589828
  12.2 7.8 %copy-start.10 = (f32[3,3]{1,0:T(4,128)S(1)}, f32[3,3]{1,0:T(4,128)}, u32[]{:S(2)}) copy-start(f32[3,3]{1,0:T(4,128)} %param.11) | copy-start | bytes 112
  13.7 12.0 %collective-permute-start.2 = (f32[64,3,10,1]{0,3,2,1:T(1,128)S(1)}, f32[64,3,10,1]{0,3,2,1:T(1,128)S(1)}, u32[]{:S(2)}, u32[]{:S(2)}) collective-permute-start(f32[64,3,10,1]{0,3,2,1:T(1,128)S(1)} %copy.43), channel_id=1, source_target_pairs={{1,0},{2,1},{3,2},{5,4},{6,5},{7,6},{9,8},{10,9},{11,10},{13,12},{... | collective-permute-start | bytes 23048 | tf_op jit(solution)/shard_map/ppermute | solution.py:20
  15.4 11.7 %collective-permute-start.3 = (f32[64,3,10,1]{0,3,2,1:T(1,128)S(1)}, f32[64,3,10,1]{0,3,2,1:T(1,128)S(1)}, u32[]{:S(2)}, u32[]{:S(2)}) collective-permute-start(f32[64,3,10,1]{0,3,2,1:T(1,128)S(1)} %copy.45), channel_id=1, source_target_pairs={{0,1},{1,2},{2,3},{4,5},{5,6},{6,7},{8,9},{9,10},{10,11},{12,13},{... | collective-permute-start | bytes 23048 | tf_op jit(solution)/shard_map/ppermute | solution.py:18
  33.4 6.4 %collective-permute-start.4 = (f32[64,3,1,256]{3,0,2,1:T(8,128)S(1)}, f32[64,3,1,256]{3,0,2,1:T(8,128)S(1)}, u32[]{:S(2)}, u32[]{:S(2)}) collective-permute-start(f32[64,3,1,256]{3,0,2,1:T(8,128)S(1)} %get-tuple-element.67), channel_id=1, source_target_pairs={{4,0},{8,4},{12,8},{5,1},{9,5},{13,9},{6,2},{10,6},{14,10},{7,3},{... | collective-permute-start | bytes 589832 | tf_op jit(solution)/shard_map/ppermute | solution.py:20
  36.7 7.0 %collective-permute-start.5 = (f32[64,3,1,256]{3,0,2,1:T(8,128)S(1)}, f32[64,3,1,256]{3,0,2,1:T(8,128)S(1)}, u32[]{:S(2)}, u32[]{:S(2)}) collective-permute-start(f32[64,3,1,256]{3,0,2,1:T(8,128)S(1)} %get-tuple-element.66), channel_id=1, source_target_pairs={{0,4},{4,8},{8,12},{1,5},{5,9},{9,13},{2,6},{6,10},{10,14},{3,7},{... | collective-permute-start | bytes 589832 | tf_op jit(solution)/shard_map/ppermute | solution.py:18
  39.8 4.0 %copy-start.7 = (f32[64,3,1,256]{3,0,2,1:T(8,128)}, f32[64,3,1,256]{3,0,2,1:T(8,128)S(1)}, u32[]{:S(2)}) copy-start(f32[64,3,1,256]{3,0,2,1:T(8,128)S(1)} %collective-permute-done.4) | copy-start | bytes 589828
  43.7 0.7 copy-start.8
  45.7 8.0 %collective-permute-start.6 = (f32[64,3,10,1]{0,3,2,1:T(1,128)}, f32[64,3,10,1]{0,3,2,1:T(1,128)S(1)}, u32[]{:S(2)}, u32[]{:S(2)}) collective-permute-start(f32[64,3,10,1]{0,3,2,1:T(1,128)} %copy.52), channel_id=1, source_target_pairs={{1,0},{2,1},{3,2},{5,4},{6,5},{7,6},{9,8},{10,9},{11,10},{13,12},{... | collective-permute-start | bytes 23048 | tf_op jit(solution)/shard_map/ppermute | solution.py:20
  47.3 6.8 %collective-permute-start.7 = (f32[64,3,10,1]{0,3,2,1:T(1,128)S(1)}, f32[64,3,10,1]{0,3,2,1:T(1,128)}, u32[]{:S(2)}, u32[]{:S(2)}) collective-permute-start(f32[64,3,10,1]{0,3,2,1:T(1,128)S(1)} %copy.54), channel_id=1, source_target_pairs={{0,1},{1,2},{2,3},{4,5},{5,6},{6,7},{8,9},{9,10},{10,11},{12,13},{... | collective-permute-start | bytes 23048 | tf_op jit(solution)/shard_map/ppermute | solution.py:18
  53.7 1.5 %copy-start.16 = (f32[3]{0:T(128)S(1)}, f32[3]{0:T(128)}, u32[]{:S(2)}) copy-start(f32[3]{0:T(128)} %get-tuple-element.45) | copy-start | bytes 40
  53.7 1.5 %copy-start.17 = (f32[3]{0:T(128)S(1)}, f32[3]{0:T(128)}, u32[]{:S(2)}) copy-start(f32[3]{0:T(128)} %get-tuple-element.46) | copy-start | bytes 40
  61.9 7.6 %copy-start.11 = (pred[2048]{0:T(1024)(128)(4,1)S(1)}, pred[2048]{0:T(1024)(128)(4,1)}, u32[]{:S(2)}) copy-start(pred[2048]{0:T(1024)(128)(4,1)} %compare_and_fusion) | copy-start | bytes 6148
  61.9 9.6 %copy-start.14 = (f32[1,1,2048]{2,1,0:T(1,128)S(1)}, f32[1,1,2048]{2,1,0:T(1,128)}, u32[]{:S(2)}) copy-start(f32[1,1,2048]{2,1,0:T(1,128)} %param.15) | copy-start | bytes 24580
  62.0 9.6 %copy-start.15 = (f32[1,1,2048]{2,1,0:T(1,128)S(1)}, f32[1,1,2048]{2,1,0:T(1,128)}, u32[]{:S(2)}) copy-start(f32[1,1,2048]{2,1,0:T(1,128)} %param.14) | copy-start | bytes 24580
  69.6 7.4 %copy-start.3 = (f32[2048,64]{1,0:T(8,128)S(1)}, f32[2048,64]{1,0:T(8,128)}, u32[]{:S(2)}) copy-start(f32[2048,64]{1,0:T(8,128)} %gather_fusion) | copy-start | bytes 1572868
  69.6 40.6 %copy-start.4 = (f32[64,64]{1,0:T(8,128)S(1)}, f32[64,64]{1,0:T(8,128)}, u32[]{:S(2)}) copy-start(f32[64,64]{1,0:T(8,128)} %fusion.34) | copy-start | bytes 49156
  77.0 36.5 %copy-start.9 = (f32[3,8,256]{2,1,0:T(8,128)S(1)}, f32[3,8,256]{2,1,0:T(8,128)}, u32[]{:S(2)}) copy-start(f32[3,8,256]{2,1,0:T(8,128)} %get-tuple-element.60) | copy-start | bytes 73732
  77.0 36.5 %copy-start.1 = (f32[64,3,8,256]{3,0,2,1:T(8,128)S(1)}, f32[64,3,8,256]{3,0,2,1:T(8,128)}, u32[]{:S(2)}) copy-start(f32[64,3,8,256]{3,0,2,1:T(8,128)} %get-tuple-element.61) | copy-start | bytes 4718596
